TPU v7x, 256 devices: a whole 4x4x8 slice. The times are simulated.
256 devices in a mesh: adapter: 32 (over z, y), tensor: 8 (over x, core).
Axes of the slice: x: 4, y: 4, z: 8, core: 2. Of those that a mesh axis runs over, the one named last changes fastest.
Arguments:
- queries: bfloat16 [4096, 4, 4096], P('adapter', None, 'tensor'), may hold values from -160 to 160
- shared_prefix_cache: bfloat16 [2, 64, 2048, 1024], P(None, 'adapter', None, 'tensor'), may hold values from -6 to 6
- rollout_suffix_cache: bfloat16 [2, 4096, 32, 1024], P(None, 'adapter', None, 'tensor'), may hold values from -9 to 9
- fresh_key_value: bfloat16 [2, 4096, 4, 1024], P(None, 'adapter', None, 'tensor'), may hold values from -9 to 9
- rollout_prefix_index: int32 [4096], P('adapter'), may hold values from 0 to 63, as said below
- rollout_suffix_length: int32 [4096], P('adapter'), may hold values from 1 to 32, as said below
- rollout_adapter_index: int32 [4096, 1], P('adapter'), may hold values from 0 to 127; in each aligned block of 128 rows (0 to 127, 128 to 255, ...) at most 5 rows name the same one
- output_projection_weight: bfloat16 [4096, 4096], P('tensor'), may hold values from -0.75 to 0.75
- adapter_shrink_weight: bfloat16 [128, 64, 4096], P('adapter', None, 'tensor'), may hold values from -0.75 to 0.75
- adapter_expand_weight: bfloat16 [128, 64, 4096], P('adapter', None, 'tensor'), may hold values from -0.75 to 0.75
Outputs:
- mixed: bfloat16 [4096, 4, 4096], P('adapter', None, 'tensor')
Inputs may be any that keep to these rules, and one draw needn't show every extreme that they name: rollout_prefix_index[r] // 2 == r // 128: a rollout's prefix is held with it, and the rollouts of one device name each of its 2 prefixes. `rollout_suffix_length`: among the rollouts of one device some has generated 32 tokens. `rollout_adapter_index`: within the rollouts of one device (aligned blocks of 128 rows) no adapter is named more than 5 times, a bound that some block reaches.
All inputs are finite; a program needn't handle non-finite values.
Results may differ from a plain program's by a relative error of at most 0.015.
Values may be sent and summed in bfloat16 or wider, within the bound.
A program may use at most 128 MiB of HBM per device.

v0:
```python
import functools, math
import jax
import jax.numpy as jnp
from jax import lax
from jax.experimental import pallas as pl
from jax.experimental.pallas import tpu as pltpu
from jax.sharding import PartitionSpec as P

HEAD = 128
NT = (((1,), (1,)), ((), ()))
F32 = jnp.float32
BF = jnp.bfloat16
MOST = 5


def row_columns(row_ref):
    values = row_ref[...].astype(F32).astype(BF)
    pick = lax.broadcasted_iota(jnp.int32, (512, 128), 0) // 4 == lax.broadcasted_iota(
        jnp.int32, (512, 128), 1
    )
    spread = jnp.where(pick, jnp.broadcast_to(values.astype(F32), (512, 128)), 0.0).astype(BF)
    return jnp.dot(spread, jnp.ones((128, 128), BF), preferred_element_type=F32)


def attend_chunk(base, q_ref, kp, vp, suf, fresh, pcol, lcol, out_ref):
    factor = (HEAD ** -0.5) * math.log2(math.e)
    subs = []
    for sub in range(2):
        row = base + sub * 32
        for h in range(4):
            subs.append(q_ref[row // 4 : row // 4 + 8, :, h * HEAD : (h + 1) * HEAD].reshape(32, HEAD))
    q = jnp.concatenate(subs, axis=0)
    pc = jnp.concatenate(
        [pcol[base + sub * 32 : base + sub * 32 + 32, :] for sub in range(2) for h in range(4)], axis=0
    )
    second = pc > 0.5
    zero = jnp.zeros_like(q)
    wide = jnp.concatenate([jnp.where(second, zero, q), jnp.where(second, q, zero)], axis=1)
    scores = lax.dot_general(wide, kp[...], NT, preferred_element_type=F32)
    top = jnp.max(scores, axis=1, keepdims=True)
    rows_i = lax.broadcasted_iota(jnp.int32, (128, 256), 0)
    keys_i = lax.broadcasted_iota(jnp.int32, (128, 256), 1)
    same = (rows_i % 32) // 4 == keys_i // 32
    kpos = (keys_i % 32).astype(F32)
    rows_f = lax.broadcasted_iota(jnp.int32, (128, 32), 0)
    keys_f = lax.broadcasted_iota(jnp.int32, (128, 32), 1)
    fmask = ((rows_f % 32) // 4 == keys_f // 4) & (keys_f % 4 <= rows_f % 4)
    suf_scores, fresh_scores = [], []
    for sub in range(2):
        r0 = (base + sub * 32) // 4
        qs = q[sub * 128 : (sub + 1) * 128]
        ks = suf[0, r0 * 32 : r0 * 32 + 256, :]
        s = lax.dot_general(qs, ks, NT, preferred_element_type=F32)
        lc = jnp.concatenate([lcol[base + sub * 32 : base + sub * 32 + 32, :]] * 4, axis=0)
        lc = jnp.concatenate([lc, lc], axis=1)
        suf_scores.append(jnp.where(same & (kpos < lc), s, -jnp.inf))
        kf = fresh[0, r0 : r0 + 8].reshape(32, HEAD)
        f = lax.dot_general(qs, kf, NT, preferred_element_type=F32)
        fresh_scores.append(jnp.where(fmask, f, -jnp.inf))
    ssc = jnp.concatenate(suf_scores, axis=0)
    fsc = jnp.concatenate(fresh_scores, axis=0)
    top = jnp.maximum(top, jnp.maximum(jnp.max(ssc, axis=1, keepdims=True), jnp.max(fsc, axis=1, keepdims=True)))
    p = jnp.exp2((scores - top) * factor)
    ps = jnp.exp2((ssc - top) * factor)
    pf = jnp.exp2((fsc - top) * factor)
    total = (
        jnp.sum(p, axis=1, keepdims=True)
        + jnp.sum(ps, axis=1, keepdims=True)
        + jnp.sum(pf, axis=1, keepdims=True)
    )
    both = jnp.dot(p.astype(BF), vp[...], preferred_element_type=F32)
    acc = jnp.where(second, both[:, HEAD:], both[:, :HEAD])
    psb, pfb = ps.astype(BF), pf.astype(BF)
    extra = []
    for sub in range(2):
        r0 = (base + sub * 32) // 4
        vs = suf[1, r0 * 32 : r0 * 32 + 256, :]
        vf = fresh[1, r0 : r0 + 8].reshape(32, HEAD)
        e = jnp.dot(psb[sub * 128 : (sub + 1) * 128], vs, preferred_element_type=F32)
        e = e + jnp.dot(pfb[sub * 128 : (sub + 1) * 128], vf, preferred_element_type=F32)
        extra.append(e)
    acc = acc + jnp.concatenate(extra, axis=0)
    acc = (acc * (1.0 / total)).astype(BF)
    for sub in range(2):
        for h in range(4):
            out_ref[base + sub * 32 : base + sub * 32 + 32, h * HEAD : (h + 1) * HEAD] = acc[
                sub * 128 + h * 32 : sub * 128 + h * 32 + 32
            ]


def attention_kernel(pfx_ref, len_ref, q_ref, prefix, suf, fresh, out_ref, kp, vp, pcol, lcol, sem):
    copies = []
    for which, ref in enumerate((kp, vp)):
        for slot in range(2):
            copies.append(
                pltpu.make_async_copy(
                    prefix.at[which, slot],
                    ref.at[:, slot * HEAD : (slot + 1) * HEAD],
                    sem.at[which * 2 + slot],
                )
            )
    for c in copies:
        c.start()
    pcol[...] = row_columns(pfx_ref)
    lcol[...] = row_columns(len_ref)
    for c in copies:
        c.wait()
    for chunk in range(8):
        attend_chunk(chunk * 64, q_ref, kp, vp, suf, fresh, pcol, lcol, out_ref)


def attention(pfx, lens, queries, prefix, suffix, fresh):
    vm = pl.BlockSpec(memory_space=pltpu.VMEM)
    return pl.pallas_call(
        attention_kernel,
        out_shape=jax.ShapeDtypeStruct((512, 512), BF),
        in_specs=[vm, vm, vm, pl.BlockSpec(memory_space=pl.ANY), vm, vm],
        out_specs=vm,
        scratch_shapes=[
            pltpu.VMEM((2048, 256), BF),
            pltpu.VMEM((2048, 256), BF),
            pltpu.VMEM((512, 128), F32),
            pltpu.VMEM((512, 128), F32),
            pltpu.SemaphoreType.DMA((4,)),
        ],
        compiler_params=pltpu.CompilerParams(vmem_limit_bytes=60 << 20),
        cost_estimate=pl.CostEstimate(flops=5 * 10**9, bytes_accessed=6 * 10**6, transcendentals=4 * 10**6),
    )(pfx, lens, queries, prefix, suffix.reshape(2, 4096, HEAD), fresh)


def head_total(attention_output, output_projection_weight):
    roll_count, step_count, width_here = attention_output.shape
    partial_sum = jnp.dot(
        attention_output.reshape(roll_count * step_count, width_here),
        output_projection_weight,
        preferred_element_type=jnp.float32,
    )
    return lax.psum_scatter(
        partial_sum.astype(jnp.bfloat16), "tensor", scatter_dimension=1, tiled=True
    ).astype(jnp.float32)


def adapter_share(
    attention_output, rollout_adapter_index, adapter_shrink_weight, adapter_expand_weight
):
    roll_count, step_count, width_here = attention_output.shape
    adapter_index = rollout_adapter_index[:, 0]
    axis_count = lax.axis_size("adapter")
    resident_adapters = adapter_shrink_weight.shape[0]
    adapter_total = resident_adapters * axis_count
    output_width = adapter_expand_weight.shape[2]
    one_hot = (
        adapter_index[:, None] == jnp.arange(adapter_total, dtype=jnp.int32)[None, :]
    ).astype(jnp.int32)
    earlier = jnp.cumsum(one_hot, axis=0) - one_hot
    slot_index = adapter_index * MOST + jnp.sum(earlier * one_hot, axis=1)
    payload = attention_output.reshape(roll_count, step_count * width_here)
    outgoing = (
        jnp.zeros((adapter_total * MOST, step_count * width_here), jnp.bfloat16)
        .at[slot_index]
        .set(payload)
    )
    received = lax.all_to_all(
        outgoing.reshape(axis_count, resident_adapters, MOST, step_count * width_here),
        "adapter",
        split_axis=0,
        concat_axis=0,
        tiled=True,
    )
    sources, owned, slots, packed = received.shape
    block_list = received.reshape(sources, owned, slots, step_count, width_here)
    shrink_step = jnp.einsum(
        "jcoxy,cqy->jcoxq", block_list, adapter_shrink_weight, preferred_element_type=jnp.float32
    )
    rank_features = lax.psum(shrink_step.astype(jnp.bfloat16), "tensor")
    expanded = jnp.einsum(
        "jzuvt,ztq->jzuvq", rank_features, adapter_expand_weight, preferred_element_type=jnp.float32
    ).astype(jnp.bfloat16)
    returned = lax.all_to_all(
        expanded.reshape(sources, owned, slots, step_count * output_width),
        "adapter",
        split_axis=0,
        concat_axis=0,
        tiled=True,
    )
    return returned.reshape(adapter_total * MOST, step_count, output_width)[slot_index]


def local(
    queries,
    shared_prefix_cache,
    rollout_suffix_cache,
    fresh_key_value,
    rollout_prefix_index,
    rollout_suffix_length,
    rollout_adapter_index,
    output_projection_weight,
    adapter_shrink_weight,
    adapter_expand_weight,
):
    roll_count, step_count, width_here = queries.shape
    prefix_count = shared_prefix_cache.shape[1]
    local_prefix = rollout_prefix_index - lax.axis_index("adapter") * prefix_count
    attention_output = attention(
        local_prefix.reshape(1, roll_count),
        rollout_suffix_length.reshape(1, roll_count),
        queries,
        shared_prefix_cache,
        rollout_suffix_cache,
        fresh_key_value,
    ).reshape(roll_count, step_count, width_here)
    output_width = adapter_expand_weight.shape[2]
    adapter_correction = adapter_share(
        attention_output, rollout_adapter_index, adapter_shrink_weight, adapter_expand_weight
    )
    base_sum = head_total(attention_output, output_projection_weight)
    mixed = base_sum.reshape(roll_count, step_count, output_width) + adapter_correction.astype(
        jnp.float32
    )
    return mixed.astype(jnp.bfloat16)


def solution(mesh):
    placed = (
        P("adapter", None, "tensor"),
        P(None, "adapter", None, "tensor"),
        P(None, "adapter", None, "tensor"),
        P(None, "adapter", None, "tensor"),
        P("adapter"),
        P("adapter"),
        P("adapter", None),
        P("tensor", None),
        P("adapter", None, "tensor"),
        P("adapter", None, "tensor"),
    )
    return jax.shard_map(
        local, mesh=mesh, in_specs=placed, out_specs=P("adapter", None, "tensor"), check_vma=False
    )
```

profile of v0, /device:TPU:8, one launch (start us, length us, event | category | flops | bytes accessed | tf_op | source)
XLA Modules:
  0.0 277.6 jit_solution(7074754781523659208)
XLA Ops:
  6.5 0.8 fusion.12
  7.5 0.8 select_reduce_fusion
  9.0 1.2 subtract_bitcast_fusion.pfx_ref
  10.2 12.1 %shard_map.100 = bf16[512,512]{1,0:T(8,128)(2,1)} custom-call(s32[1,128]{1,0:T(1,128)} %subtract_bitcast_fusion.pfx_ref, s32[1,128]{1,0:T(1,128)} %bitcast.35, bf16[128,4,512]{2,1,0:T(4,128)(2,1)} %q_ref.1, bf16[2,2,2048,128]{3,2,1,0:T(8,128)(2,1)} %prefix.1, bf16[2,4096,128]{2,1,0:T(8,128)(2,1)} %bitcast.34, bf16[2,128,4,128]{3,2,1,0:T(4,128)(2,1)} %fresh.1), custom_call_target="tpu_custom_call" | custom-call | flops 5000000000 | bytes 6000000 | tf_op jit(solution)/shard_map/pallas_call | solution.py:114
  22.4 1.4 reshape.51
  23.7 2.5 scatter_custom_fusion
  26.3 2.9 %reshape.33 = bf16[32,4,5,2048]{3,2,1,0:T(8,128)(2,1)} reshape(bf16[640,2048]{1,0:T(8,128)(2,1)S(1)} %scatter_custom_fusion) | data formatting | bytes 5242880 | tf_op jit(solution)/shard_map/reshape | solution.py:164
  29.1 5.1 %copy.19 = bf16[32,4,5,2048]{3,1,2,0:T(4,128)(2,1)S(1)} copy(bf16[32,4,5,2048]{3,2,1,0:T(8,128)(2,1)} %reshape.33) | data formatting | bytes 5242880 | tf_op jit(solution)/shard_map/reshape | solution.py:164
  34.2 73.3 %all_to_all.10 = bf16[32,4,5,2048]{3,1,2,0:T(4,128)(2,1)S(1)} all-to-all(bf16[32,4,5,2048]{3,1,2,0:T(4,128)(2,1)S(1)} %copy.19), channel_id=1, replica_groups=mesh['adapter'=32,'tensor'=8] {'adapter'}, dimensions={0} | all-to-all | bytes 5242880 | tf_op jit(solution)/shard_map/all_to_all | solution.py:163
  107.5 3.4 %reshape.57 = bf16[32,4,5,4,512]{4,3,1,2,0:T(4,128)(2,1)} reshape(bf16[32,4,5,2048]{3,1,2,0:T(4,128)(2,1)S(1)} %all_to_all.10) | data formatting | bytes 5242880 | tf_op jit(solution)/shard_map/reshape | solution.py:171
  110.9 4.5 %fusion.7 = bf16[32,4,5,4,64]{4,0,3,2,1:T(8,128)(2,1)} fusion(bf16[32,4,5,4,512]{4,3,1,2,0:T(4,128)(2,1)} %reshape.57, bf16[4,64,512]{2,1,0:T(8,128)(2,1)S(1)} %copy-done.3), kind=kOutput, calls=%fused_computation.9 | convolution fusion | flops 167936000 | bytes 3211264 | tf_op jit(solution)/shard_map/jcoxy,cqy->jcoxq/dot_general | solution.py:172
  115.5 6.5 %convolution_convert_fusion = bf16[512,4096]{1,0:T(8,128)(2,1)} fusion(bf16[512,512]{1,0:T(8,128)(2,1)S(1)} %copy-done.2, bf16[512,4096]{1,0:T(8,128)(2,1)} %param.17), kind=kOutput, calls=%fused_computation.2 | convolution fusion | flops 2149580800 | bytes 8912896 | tf_op jit(solution)/shard_map/dot_general | solution.py:133
  122.0 56.9 %all-reduce.2.cloned.1.call-done = bf16[32,4,5,4,64]{4,0,3,2,1:T(8,128)(2,1)} async-done(((bf16[32,4,5,4,64]{4,0,3,2,1:T(8,128)(2,1)}), bf16[32,4,5,4,64]{4,0,3,2,1:T(8,128)(2,1)}) %all-reduce.2.cloned.1.call-update) | async-done | bytes 327696 | tf_op jit(solution)/shard_map/psum | solution.py:175
  178.9 1.9 convert_bitcast_fusion
  180.8 2.0 copy.29
  182.8 3.4 %reshape.58 = bf16[32,4,5,2048]{3,1,2,0:T(4,128)(2,1)} reshape(bf16[32,4,5,4,512]{4,3,1,2,0:T(4,128)(2,1)S(1)} %copy.29) | data formatting | bytes 5242880 | tf_op jit(solution)/shard_map/reshape | solution.py:180
  186.3 10.2 %all-to-all-start.1 = ((bf16[32,4,5,2048]{3,1,2,0:T(4,128)(2,1)}), bf16[32,4,5,2048]{3,1,2,0:T(4,128)(2,1)S(1)}, u32[]{:S(2)}, u32[]{:S(2)}) async-start(bf16[32,4,5,2048]{3,1,2,0:T(4,128)(2,1)} %reshape.58), calls=%async_computation.2 | async-start | bytes 5242880 | tf_op jit(solution)/shard_map/all_to_all | solution.py:179
  196.5 25.2 %reduce-scatter.2.cloned.1.call-done = bf16[512,512]{1,0:T(8,128)(2,1)} async-done(((bf16[512,4096]{1,0:T(8,128)(2,1)}), bf16[512,512]{1,0:T(8,128)(2,1)}) %reduce-scatter.2.cloned.1.call-update) | async-done | bytes 524304 | tf_op jit(solution)/shard_map/reduce_scatter | solution.py:138
  221.6 2.3 reshape.38
  224.0 31.3 %all-to-all-done.1 = bf16[32,4,5,2048]{3,1,2,0:T(4,128)(2,1)S(1)} async-done(((bf16[32,4,5,2048]{3,1,2,0:T(4,128)(2,1)}), bf16[32,4,5,2048]{3,1,2,0:T(4,128)(2,1)S(1)}, u32[]{:S(2)}, u32[]{:S(2)}) %all-to-all-start.1) | async-done | bytes 2621472 | tf_op jit(solution)/shard_map/all_to_all | solution.py:179
  255.2 3.9 %copy.24 = bf16[32,4,5,2048]{3,2,1,0:T(8,128)(2,1)} copy(bf16[32,4,5,2048]{3,1,2,0:T(4,128)(2,1)S(1)} %all-to-all-done.1) | data formatting | bytes 5242880 | tf_op jit(solution)/shard_map/all_to_all | solution.py:179
  259.2 7.8 %reshape.36 = bf16[640,4,512]{2,1,0:T(4,128)(2,1)} reshape(bf16[32,4,5,2048]{3,2,1,0:T(8,128)(2,1)} %copy.24) | data formatting | bytes 5242880 | tf_op jit(solution)/shard_map/reshape | solution.py:186
  266.9 2.8 gather_fusion
  269.7 1.1 add_convert_fusion
  (15 shorter events, 0.9 us)
Async XLA Ops:
  6.5 172.4 %copy-start = (bf16[4,64,512]{2,1,0:T(8,128)(2,1)S(1)}, bf16[4,64,512]{2,1,0:T(8,128)(2,1)}, u32[]{:S(2)}) copy-start(bf16[4,64,512]{2,1,0:T(8,128)(2,1)} %param.19) | copy-start | bytes 786436
  6.5 172.4 %all-reduce.2.cloned.1.call-start = ((), (), s32[]{:S(2)}) async-start(), calls=%async_computation.4 | async-start | bytes 1310720 | tf_op jit(solution)/shard_map/psum | solution.py:175
  107.5 3.4 %copy-start.3 = (bf16[4,64,512]{2,1,0:T(8,128)(2,1)S(1)}, bf16[4,64,512]{2,1,0:T(8,128)(2,1)}, u32[]{:S(2)}) copy-start(bf16[4,64,512]{2,1,0:T(8,128)(2,1)} %param.18) | copy-start | bytes 786436
  110.9 4.6 %copy-start.2 = (bf16[512,512]{1,0:T(8,128)(2,1)S(1)}, bf16[512,512]{1,0:T(8,128)(2,1)}, u32[]{:S(2)}) copy-start(bf16[512,512]{1,0:T(8,128)(2,1)} %shard_map.100) | copy-start | bytes 1572868
  115.4 106.2 %reduce-scatter.2.cloned.1.call-start = ((), (), s32[]{:S(2)}) async-start(), calls=%async_computation.3 | async-start | bytes 4718592 | tf_op jit(solution)/shard_map/reduce_scatter | solution.py:138
  186.3 69.0 %all-to-all-start.1 = ((bf16[32,4,5,2048]{3,1,2,0:T(4,128)(2,1)}), bf16[32,4,5,2048]{3,1,2,0:T(4,128)(2,1)S(1)}, u32[]{:S(2)}, u32[]{:S(2)}) async-start(bf16[32,4,5,2048]{3,1,2,0:T(4,128)(2,1)} %reshape.58), calls=%async_computation.2 | async-start | bytes 5242880 | tf_op jit(solution)/shard_map/all_to_all | solution.py:179
  259.2 10.5 %copy-start.1 = (f32[128,4,512]{2,1,0:T(4,128)S(1)}, f32[128,4,512]{2,1,0:T(4,128)}, u32[]{:S(2)}) copy-start(f32[128,4,512]{2,1,0:T(4,128)} %reshape.38) | copy-start | bytes 3145732
Sparse Core Ops, SparseCore 0:
  115.5 63.3 all-reduce.1
  181.5 40.1 reduce-scatter.1
where the time goes:
time: 280 us; the launch traced here: 278 us
  waiting for transfers between devices  113 us (40%)
  blocking collectives  73.3 us (26%)
  local copies, waits for them, and re-layouts  37.5 us (13%)
  between operations  13.5 us (5%)
  matrix products  12.8 us (5%)
  Pallas kernels  12.1 us (4%)
  starting transfers between devices  10.2 us (4%)
  other arithmetic  4.76 us (2%)
    all_to_all x1, blocking collectives, adapter_share(): lax.all_to_all(outgoing.reshape(axis_count, resident_adapters, MOST, step...  73.3 us
    psum x1, waiting for transfers between devices, adapter_share(): rank_features = lax.psum(shrink_step.astype(jnp.bfloat16), 'tensor')  56.9 us
    all_to_all x1, waiting for transfers between devices, adapter_share(): lax.all_to_all(expanded.reshape(sources, owned, slots, step_count * outpu...  31.3 us
    reduce_scatter x1, waiting for transfers between devices, head_total(): lax.psum_scatter(partial_sum.astype(jnp.bfloat16), 'tensor', scatter_dime...  25.2 us
    pallas_call x1, Pallas kernels, attention(): pl.pallas_call(attention_kernel, out_shape=jax.ShapeDtypeStruct((512, 512...  12.1 us
    all_to_all x1, starting transfers between devices, adapter_share(): lax.all_to_all(expanded.reshape(sources, owned, slots, step_count * outpu...  10.2 us
    reshape x2, local copies, waits for them, and re-layouts, adapter_share(): outgoing.reshape(axis_count, resident_adapters, MOST, step_count * width_...  7.95 us
    reshape x1, local copies, waits for them, and re-layouts, adapter_share(): returned.reshape(adapter_total * MOST, step_count, output_width)[slot_index]  7.76 us
  transfers between devices with their start and end apart: 3, of which 3 were waited for; matrix products, arithmetic and copies ran while one was open for 6% of the time, Pallas kernels for 0%

commit v1 on v0

v1 whole, which is shorter than its diff:
```python
import math
import jax
import jax.numpy as jnp
from jax import lax
from jax.experimental import pallas as pl
from jax.experimental.pallas import tpu as pltpu
from jax.sharding import PartitionSpec as P

HEAD = 128
NT = (((1,), (1,)), ((), ()))
F32 = jnp.float32
BF = jnp.bfloat16


def row_columns(row_ref):
    values = row_ref[...].astype(F32).astype(BF)
    pick = lax.broadcasted_iota(jnp.int32, (512, 128), 0) // 4 == lax.broadcasted_iota(
        jnp.int32, (512, 128), 1
    )
    spread = jnp.where(pick, jnp.broadcast_to(values.astype(F32), (512, 128)), 0.0).astype(BF)
    return jnp.dot(spread, jnp.ones((128, 128), BF), preferred_element_type=F32)


def attend_chunk(base, q_ref, kp, vp, suf, fresh, pcol, lcol, out_ref):
    factor = (HEAD ** -0.5) * math.log2(math.e)
    subs = []
    for sub in range(2):
        row = base + sub * 32
        for h in range(4):
            subs.append(q_ref[row // 4 : row // 4 + 8, :, h * HEAD : (h + 1) * HEAD].reshape(32, HEAD))
    q = jnp.concatenate(subs, axis=0)
    pc = jnp.concatenate(
        [pcol[base + sub * 32 : base + sub * 32 + 32, :] for sub in range(2) for h in range(4)], axis=0
    )
    second = pc > 0.5
    zero = jnp.zeros_like(q)
    wide = jnp.concatenate([jnp.where(second, zero, q), jnp.where(second, q, zero)], axis=1)
    scores = lax.dot_general(wide, kp[...], NT, preferred_element_type=F32)
    top = jnp.max(scores, axis=1, keepdims=True)
    rows_i = lax.broadcasted_iota(jnp.int32, (128, 256), 0)
    keys_i = lax.broadcasted_iota(jnp.int32, (128, 256), 1)
    same = (rows_i % 32) // 4 == keys_i // 32
    kpos = (keys_i % 32).astype(F32)
    rows_f = lax.broadcasted_iota(jnp.int32, (128, 32), 0)
    keys_f = lax.broadcasted_iota(jnp.int32, (128, 32), 1)
    fmask = ((rows_f % 32) // 4 == keys_f // 4) & (keys_f % 4 <= rows_f % 4)
    suf_scores, fresh_scores = [], []
    for sub in range(2):
        r0 = (base + sub * 32) // 4
        qs = q[sub * 128 : (sub + 1) * 128]
        ks = suf[0, r0 * 32 : r0 * 32 + 256, :]
        s = lax.dot_general(qs, ks, NT, preferred_element_type=F32)
        lc = jnp.concatenate([lcol[base + sub * 32 : base + sub * 32 + 32, :]] * 4, axis=0)
        lc = jnp.concatenate([lc, lc], axis=1)
        suf_scores.append(jnp.where(same & (kpos < lc), s, -jnp.inf))
        kf = fresh[0, r0 : r0 + 8].reshape(32, HEAD)
        f = lax.dot_general(qs, kf, NT, preferred_element_type=F32)
        fresh_scores.append(jnp.where(fmask, f, -jnp.inf))
    ssc = jnp.concatenate(suf_scores, axis=0)
    fsc = jnp.concatenate(fresh_scores, axis=0)
    top = jnp.maximum(top, jnp.maximum(jnp.max(ssc, axis=1, keepdims=True), jnp.max(fsc, axis=1, keepdims=True)))
    p = jnp.exp2((scores - top) * factor)
    ps = jnp.exp2((ssc - top) * factor)
    pf = jnp.exp2((fsc - top) * factor)
    total = (
        jnp.sum(p, axis=1, keepdims=True)
        + jnp.sum(ps, axis=1, keepdims=True)
        + jnp.sum(pf, axis=1, keepdims=True)
    )
    both = jnp.dot(p.astype(BF), vp[...], preferred_element_type=F32)
    acc = jnp.where(second, both[:, HEAD:], both[:, :HEAD])
    psb, pfb = ps.astype(BF), pf.astype(BF)
    extra = []
    for sub in range(2):
        r0 = (base + sub * 32) // 4
        vs = suf[1, r0 * 32 : r0 * 32 + 256, :]
        vf = fresh[1, r0 : r0 + 8].reshape(32, HEAD)
        e = jnp.dot(psb[sub * 128 : (sub + 1) * 128], vs, preferred_element_type=F32)
        e = e + jnp.dot(pfb[sub * 128 : (sub + 1) * 128], vf, preferred_element_type=F32)
        extra.append(e)
    acc = acc + jnp.concatenate(extra, axis=0)
    acc = (acc * (1.0 / total)).astype(BF)
    for sub in range(2):
        for h in range(4):
            out_ref[base + sub * 32 : base + sub * 32 + 32, h * HEAD : (h + 1) * HEAD] = acc[
                sub * 128 + h * 32 : sub * 128 + h * 32 + 32
            ]


NMSG = 256
MESHID = pl.DeviceIdType.MESH


class Net:
    def __init__(self, ssem, rsem):
        self.ssem, self.rsem, self.sent, self.count = ssem, rsem, [], 0

    def copy(self, src, dst, device):
        i = self.count
        self.count += 1
        d = pltpu.make_async_remote_copy(
            src_ref=src,
            dst_ref=dst,
            send_sem=self.ssem.at[i],
            recv_sem=self.rsem.at[i],
            device_id=device,
            device_id_type=MESHID,
        )
        self.sent.append(d)
        return d


def mega_kernel(
    pfx_ref, len_ref, idx_ref, q_ref, prefix, suf, fresh, wo_hbm, a_hbm, b_hbm,
    out_ref,
    kp, vp, pcol, lcol, wo, ag, bg0, bg1, att, fl, fr, fo, part, pr, s1, s2, s3,
    t2l, t2r, f1l, f3r, idn, idc, acc, cp, cr, cs, cf, xs, e0, e1, ol, orr, eR, eL, dl, dr,
    lsem, ssem, rsem,
):
    a, t = lax.axis_index("adapter"), lax.axis_index("tensor")
    z, y, x, c = a // 4, a % 4, t // 2, t % 2
    zr, zl = (((z + 1) % 8) * 4 + y, t), (((z + 7) % 8) * 4 + y, t)
    yr, yl, yo = (z * 4 + (y + 1) % 4, t), (z * 4 + (y + 3) % 4, t), (z * 4 + (y + 2) % 4, t)
    xr, xl, pc = (a, ((x + 1) % 4) * 2 + c), (a, ((x + 3) % 4) * 2 + c), (a, x * 2 + (1 - c))
    peers = [(a, (t + d) % 8) for d in range(1, 8)]
    net = Net(ssem, rsem)

    barrier = pltpu.get_barrier_semaphore()
    everyone = [zr, zl, yr, yl, yo] + peers
    for dev in everyone:
        pl.semaphore_signal(barrier, inc=1, device_id=dev, device_id_type=MESHID)

    loads, nl = {}, 0

    def load(name, src, dst):
        nonlocal nl
        d = pltpu.make_async_copy(src, dst, lsem.at[nl])
        nl += 1
        loads.setdefault(name, []).append(d)
        d.start()

    def loaded(name):
        for d in loads[name]:
            d.wait()

    for which, ref in enumerate((kp, vp)):
        for slot in range(2):
            load("kv", prefix.at[which, slot], ref.at[:, slot * HEAD : (slot + 1) * HEAD])
    load("a", a_hbm, ag.at[0])
    for j in range(8):
        dest = ((x + j % 4) % 4) * 2 + (c + j // 4) % 2
        load("wo", wo_hbm.at[:, pl.ds(pl.multiple_of(dest * 512, 512), 512)], wo.at[j])
    load("b", b_hbm.at[:, 0:256], bg0.at[0])
    load("b", b_hbm.at[:, 256:512], bg1.at[0])

    own = [a_hbm, b_hbm.at[:, 0:256], b_hbm.at[:, 256:512]]
    store = [ag, bg0, bg1]
    last = {(0, 0): 4, (0, 1): 3, (1, 0): 3, (1, 1): 4}
    hops = {}
    for mat in range(3):
        for h in range(2):
            rows = slice(h * 128, h * 128 + 128)
            for way in range(2):
                for k in range(1, last[(way, h)] + 1):
                    here = (8 - (k - 1)) % 8 if way == 0 else k - 1
                    there = (8 - k) % 8 if way == 0 else k
                    src = own[mat].at[rows] if k == 1 else store[mat].at[here, rows]
                    hops[mat, h, way, k] = net.copy(src, store[mat].at[there, rows], zr if way == 0 else zl)

    def z_first(mat):
        for h in range(2):
            for way in range(2):
                hops[mat, h, way, 1].start()

    def z_step(mat, h, k):
        for way in range(2):
            if k <= last[(way, h)]:
                hops[mat, h, way, k].wait_recv()
                if k < last[(way, h)]:
                    hops[mat, h, way, k + 1].start()

    id_msgs = [
        net.copy(idx_ref, idn.at[0], yr),
        net.copy(idx_ref, idn.at[1], yl),
        net.copy(idx_ref, idn.at[2], yo),
    ]
    pl.semaphore_wait(barrier, len(everyone))
    z_first(0)
    for d in id_msgs:
        d.start()

    pcol[...] = row_columns(pfx_ref)
    lcol[...] = row_columns(len_ref)
    idc[0] = row_columns(idx_ref)

    feat = {}
    for m in range(4):
        rows, ha, hb = slice(m * 128, m * 128 + 128), slice(m * 128, m * 128 + 64), slice(m * 128 + 64, m * 128 + 128)
        feat["r", m] = net.copy(att.at[rows], fl.at[rows], yr)
        feat["l", m] = net.copy(att.at[rows], fr.at[rows], yl)
        feat["rr", m] = net.copy(fl.at[ha], fo.at[ha], yr)
        feat["ll", m] = net.copy(fr.at[hb], fo.at[hb], yl)
    base = {}
    for m in range(4):
        rows, ha, hb = slice(m * 128, m * 128 + 128), slice(m * 128, m * 128 + 64), slice(m * 128 + 64, m * 128 + 128)
        base["p", m] = net.copy(part.at[1, :, rows], pr.at[:, rows], pc)
        base["2r", m] = net.copy(s2.at[ha], t2l.at[ha], xr)
        base["2l", m] = net.copy(s2.at[hb], t2r.at[hb], xl)
        base["1r", m] = net.copy(s1.at[rows], f1l.at[rows], xr)
        base["1l", m] = net.copy(s3.at[rows], f3r.at[rows], xl)

    def project(m):
        rows = slice(m * 128, m * 128 + 128)
        here = att[rows, :]
        for j in (4, 5, 6, 7, 2, 1, 3, 0):
            got = jnp.dot(here, wo[j], preferred_element_type=F32)
            part[j // 4, j % 4, rows, :] = got.astype(BF)
            if j == 7:
                base["p", m].start()

    def forward_features(m):
        feat["r", m].wait_recv()
        feat["rr", m].start()
        feat["l", m].wait_recv()
        feat["ll", m].start()

    def paired(dx, rows):
        return part[0, dx, rows, :].astype(F32) + pr[dx, rows, :].astype(F32)

    def base_two(m):
        base["p", m].wait_recv()
        rows = slice(m * 128, m * 128 + 128)
        s2[rows, :] = paired(2, rows).astype(BF)
        base["2r", m].start()
        base["2l", m].start()

    def base_one(m):
        ha, hb = slice(m * 128, m * 128 + 64), slice(m * 128 + 64, m * 128 + 128)
        base["2r", m].wait_recv()
        s1[ha, :] = (paired(1, ha) + t2l[ha, :].astype(F32)).astype(BF)
        s1[hb, :] = paired(1, hb).astype(BF)
        base["1r", m].start()
        base["2l", m].wait_recv()
        s3[ha, :] = paired(3, ha).astype(BF)
        s3[hb, :] = (paired(3, hb) + t2r[hb, :].astype(F32)).astype(BF)
        base["1l", m].start()

    feats = [att, fl, fr, fo]
    low = lax.broadcasted_iota(jnp.int32, (512, 128), 1) < 64
    lowh = lax.broadcasted_iota(jnp.int32, (256, 128), 1) < 64

    def lane_adapter(g):
        first = ((z + g // 2) % 8) * 16 + y * 4 + (g % 2) * 2
        lanes = lax.broadcasted_iota(jnp.int32, (1, 128), 1) // 64
        return (lanes + first).astype(F32)

    def codes(b):
        total = None
        ids = idc[b]
        for d in range(8):
            got = lax.dot_general(feats[b][...], ag[d], NT, preferred_element_type=F32)
            for half in range(2):
                mine = jnp.where(ids == lane_adapter(2 * d + half), got[:, half * 128 : half * 128 + 128], 0.0)
                total = mine if total is None else total + mine
        acc[...] = total
        folded = acc[...] + pltpu.roll(acc[...], 64, 1)
        cp[b] = jnp.where(lowh, folded[:256], folded[256:]).astype(BF)

    scat, gath = {}, {}
    for b in range(4):
        for d in range(1, 8):
            to = (t + d) % 8
            rows = pl.ds(pl.multiple_of(to * 32, 32), 32)
            scat[b, d] = net.copy(cp.at[b, rows], cr.at[b, d], (a, to))
            rows = pl.ds(pl.multiple_of(t * 32, 32), 32)
            gath[b, d] = net.copy(cs.at[b], cf.at[b, rows], (a, to))

    def scatter_codes(b):
        for d in range(1, 8):
            scat[b, d].start()

    def reduce_codes(b):
        rows = pl.ds(pl.multiple_of(t * 32, 32), 32)
        s = cp[b, rows, :].astype(F32)
        for d in range(1, 8):
            scat[b, d].wait_recv()
            s = s + cr[b, d].astype(F32)
        s = s.astype(BF)
        cs[b] = s
        cf[b, rows, :] = s
        for d in range(1, 8):
            gath[b, d].start()

    def spread_codes(b):
        for d in range(1, 8):
            gath[b, d].wait_recv()
        packed = cf[b].astype(F32)
        turned = pltpu.roll(packed, 64, 1)
        both = jnp.concatenate([jnp.where(lowh, packed, turned), jnp.where(lowh, turned, packed)], axis=0)
        ids = idc[b]
        for g in range(16):
            xs[b, :, g * 128 : g * 128 + 128] = jnp.where(ids == lane_adapter(g), both, 0.0).astype(BF)

    outs = {}
    es, bgs = [e0, e1], [bg0, bg1]
    for n in range(2):
        for m in range(2):
            rows, ha, hb = slice(m * 256, m * 256 + 256), slice(m * 256, m * 256 + 128), slice(m * 256 + 128, m * 256 + 256)
            outs["or", n, m] = net.copy(es[n].at[3, ha], ol.at[n, ha], yr)
            outs["ol", n, m] = net.copy(es[n].at[3, hb], orr.at[n, hb], yl)
            outs["r", n, m] = net.copy(eR.at[n, rows], dl.at[n, rows], yr)
            outs["l", n, m] = net.copy(eL.at[n, rows], dr.at[n, rows], yl)

    def expand(n, b):
        for m in range(2):
            rows = slice(m * 256, m * 256 + 256)
            w = jnp.reshape(bgs[n][...], (2048, 256))
            got = jnp.dot(xs[b, rows, :], w, preferred_element_type=F32)
            es[n][b, rows, :] = got.astype(BF)
            if b == 3:
                outs["or", n, m].start()
                outs["ol", n, m].start()

    def relay(n, m):
        ha, hb = slice(m * 256, m * 256 + 128), slice(m * 256 + 128, m * 256 + 256)
        e = es[n]
        outs["or", n, m].wait_recv()
        eR[n, ha, :] = e[2, ha, :] + ol[n, ha, :]
        eR[n, hb, :] = e[2, hb, :]
        outs["r", n, m].start()
        outs["ol", n, m].wait_recv()
        eL[n, ha, :] = e[1, ha, :]
        eL[n, hb, :] = e[1, hb, :] + orr[n, hb, :]
        outs["l", n, m].start()

    def finish(n, m):
        outs["r", n, m].wait_recv()
        outs["l", n, m].wait_recv()
        rows = slice(m * 256, m * 256 + 256)
        cols = slice(n * 256, n * 256 + 256)
        total = part[0, 0, rows, cols].astype(F32) + pr[0, rows, cols].astype(F32)
        total = total + f1l[rows, cols].astype(F32) + f3r[rows, cols].astype(F32)
        delta = es[n][0, rows, :].astype(F32) + dl[n, rows, :].astype(F32) + dr[n, rows, :].astype(F32)
        out_ref[m * 64 : m * 64 + 64, :, cols] = (total + delta).astype(BF).reshape(64, 4, 256)

    loaded("kv")
    steps = [(0, 0, 1), (0, 1, 1), (0, 0, 2), (0, 1, 2), (0, 0, 3), (0, 1, 3), (0, 0, 4), (0, 1, 4)]
    for m in range(4):
        for i in (2 * m, 2 * m + 1):
            attend_chunk(i * 64, q_ref, kp, vp, suf, fresh, pcol, lcol, att)
            if i >= 1:
                z_step(*steps[i - 1])
            if i == 4:
                z_first(1)
        feat["r", m].start()
        feat["l", m].start()
        if m == 0:
            loaded("wo")
        if m >= 1:
            base_two(m - 1)
            forward_features(m - 1)
        project(m)
        if m >= 1:
            base_one(m - 1)
    z_step(*steps[7])
    z_first(2)
    base_two(3)
    for n, d in enumerate(id_msgs):
        d.wait_recv()
        idc[n + 1] = row_columns(idn.at[n])
    forward_features(3)
    loaded("a")
    loaded("b")
    codes(0)
    scatter_codes(0)
    base_one(3)
    z_step(1, 0, 1)
    z_step(1, 1, 1)
    codes(1)
    scatter_codes(1)
    z_step(1, 0, 2)
    z_step(1, 1, 2)
    codes(2)
    scatter_codes(2)
    reduce_codes(0)
    z_step(2, 0, 1)
    z_step(2, 1, 1)
    reduce_codes(1)
    for m in range(4):
        feat["rr", m].wait_recv()
        feat["ll", m].wait_recv()
    codes(3)
    scatter_codes(3)
    z_step(1, 0, 3)
    z_step(1, 1, 3)
    reduce_codes(2)
    z_step(2, 0, 2)
    z_step(2, 1, 2)
    spread_codes(0)
    reduce_codes(3)
    spread_codes(1)
    z_step(1, 0, 4)
    z_step(1, 1, 4)
    spread_codes(2)
    z_step(2, 0, 3)
    z_step(2, 1, 3)
    spread_codes(3)
    expand(0, 3)
    expand(0, 2)
    expand(0, 1)
    relay(0, 0)
    relay(0, 1)
    z_step(2, 0, 4)
    z_step(2, 1, 4)
    expand(1, 3)
    expand(1, 2)
    expand(1, 1)
    relay(1, 0)
    relay(1, 1)
    expand(0, 0)
    expand(1, 0)
    for m in range(4):
        base["1r", m].wait_recv()
        base["1l", m].wait_recv()
    for n in range(2):
        for m in range(2):
            finish(n, m)
    for d in net.sent:
        d.wait_send()


def local(
    queries,
    shared_prefix_cache,
    rollout_suffix_cache,
    fresh_key_value,
    rollout_prefix_index,
    rollout_suffix_length,
    rollout_adapter_index,
    output_projection_weight,
    adapter_shrink_weight,
    adapter_expand_weight,
):
    local_prefix = rollout_prefix_index - lax.axis_index("adapter") * 2
    vm, anyspec = pl.BlockSpec(memory_space=pltpu.VMEM), pl.BlockSpec(memory_space=pl.ANY)
    V = pltpu.VMEM
    return pl.pallas_call(
        mega_kernel,
        out_shape=jax.ShapeDtypeStruct((128, 4, 512), BF),
        in_specs=[vm, vm, vm, vm, anyspec, vm, vm, anyspec, anyspec, anyspec],
        out_specs=vm,
        scratch_shapes=[
            V((2048, 256), BF), V((2048, 256), BF), V((512, 128), F32), V((512, 128), F32),
            V((8, 512, 512), BF), V((8, 256, 512), BF), V((8, 256, 256), BF), V((8, 256, 256), BF),
            V((512, 512), BF), V((512, 512), BF), V((512, 512), BF), V((512, 512), BF),
            V((2, 4, 512, 512), BF), V((4, 512, 512), BF),
            V((512, 512), BF), V((512, 512), BF), V((512, 512), BF),
            V((512, 512), BF), V((512, 512), BF), V((512, 512), BF), V((512, 512), BF),
            V((3, 1, 128), jnp.int32), V((4, 512, 128), F32), V((512, 128), F32),
            V((4, 256, 128), BF), V((4, 8, 32, 128), BF), V((4, 32, 128), BF), V((4, 256, 128), BF),
            V((4, 512, 2048), BF),
            V((4, 512, 256), BF), V((4, 512, 256), BF), V((2, 512, 256), BF), V((2, 512, 256), BF),
            V((2, 512, 256), BF), V((2, 512, 256), BF), V((2, 512, 256), BF), V((2, 512, 256), BF),
            pltpu.SemaphoreType.DMA((16,)),
            pltpu.SemaphoreType.DMA((NMSG,)),
            pltpu.SemaphoreType.DMA((NMSG,)),
        ],
        compiler_params=pltpu.CompilerParams(
            vmem_limit_bytes=62 << 20, collective_id=0, has_side_effects=True
        ),
        cost_estimate=pl.CostEstimate(flops=16 * 10**9, bytes_accessed=12 * 10**6, transcendentals=4 * 10**6),
    )(
        local_prefix.reshape(1, 128),
        rollout_suffix_length.reshape(1, 128),
        rollout_adapter_index.reshape(1, 128),
        queries,
        shared_prefix_cache,
        rollout_suffix_cache.reshape(2, 4096, HEAD),
        fresh_key_value,
        output_projection_weight,
        adapter_shrink_weight.reshape(256, 512),
        adapter_expand_weight.reshape(256, 512),
    )


def solution(mesh):
    placed = (
        P("adapter", None, "tensor"),
        P(None, "adapter", None, "tensor"),
        P(None, "adapter", None, "tensor"),
        P(None, "adapter", None, "tensor"),
        P("adapter"),
        P("adapter"),
        P("adapter", None),
        P("tensor", None),
        P("adapter", None, "tensor"),
        P("adapter", None, "tensor"),
    )
    return jax.shard_map(
        local, mesh=mesh, in_specs=placed, out_specs=P("adapter", None, "tensor"), check_vma=False
    )
```

time: 280 us -> 93.4 us (0.33)
  waiting for transfers between devices: 113 us -> 0 us
  Pallas kernels: 12.1 us -> 90.1 us
  blocking collectives: 73.3 us -> 0 us
  local copies, waits for them, and re-layouts: 37.5 us -> 2.02 us
  between operations: 13.5 us -> 0.01 us
  matrix products: 12.8 us -> 0 us
  starting transfers between devices: 10.2 us -> 0 us
  other arithmetic: 4.76 us -> 1.17 us
    pallas_call x1, Pallas kernels: 12.1 us -> 90.1 us  [local(): pl.pallas_call(mega_kernel, out_shape=jax.ShapeDtypeStruct((128, 4, 512),...]
    all_to_all x1 -> x0, blocking collectives: 73.3 us -> none  [adapter_share(): lax.all_to_all(outgoing.reshape(axis_count, resident_adapters, MOST, step...]
    psum x1 -> x0, waiting for transfers between devices: 56.9 us -> none  [adapter_share(): rank_features = lax.psum(shrink_step.astype(jnp.bfloat16), 'tensor')]
    all_to_all x1 -> x0, waiting for transfers between devices: 31.3 us -> none  [adapter_share(): lax.all_to_all(expanded.reshape(sources, owned, slots, step_count * outpu...]
    reshape x7 -> x0, local copies, waits for them, and re-layouts: 26.9 us -> none  [the longest x2 7.95 us: adapter_share(): outgoing.reshape(axis_count, resident_adapters, MOST, step_count * width_...]
    reduce_scatter x1 -> x0, waiting for transfers between devices: 25.2 us -> none  [head_total(): lax.psum_scatter(partial_sum.astype(jnp.bfloat16), 'tensor', scatter_dime...]
    dot_general x3 -> x0, matrix products: 12.8 us -> none  [the longest x1 6.47 us: head_total(): jnp.dot(attention_output.reshape(roll_count * step_count, width_here), ou...]
    all_to_all x1 -> x0, starting transfers between devices: 10.2 us -> none  [adapter_share(): lax.all_to_all(expanded.reshape(sources, owned, slots, step_count * outpu...]
  transfers between devices with their start and end apart: 3 -> 0, of which waited for: 3 -> 0; matrix products, arithmetic and copies ran while one was open for 6% -> 0% of each run, Pallas kernels for 0% -> 0%
where the time goes in v1:
time: 93.4 us; the launch traced here: 93.3 us
  Pallas kernels  90.1 us (96%)
  local copies, waits for them, and re-layouts  2.02 us (2%)
  other arithmetic  1.17 us (1%)
    pallas_call x1, Pallas kernels, local(): pl.pallas_call(mega_kernel, out_shape=jax.ShapeDtypeStruct((128, 4, 512),...  90.1 us
    unnamed x1, local copies, waits for them, and re-layouts  2.02 us

profile of v1, /device:TPU:8, one launch (start us, length us, event | category | flops | bytes accessed | tf_op | source)
XLA Modules:
  0.0 93.3 jit_solution(5450936141593871991)
XLA Ops:
  0.0 1.2 %subtract_bitcast_fusion.pfx_ref = s32[1,128]{1,0:T(1,128)} fusion(s32[128]{0:T(128)} %param.14, s32[]{:T(128)S(6)} %mul.3), kind=kLoop, calls=%fused_computation | loop fusion | flops 128 | bytes 1028 | tf_op jit(solution)/shard_map/reshape | solution.py:473
  1.2 90.1 %shard_map.100 = bf16[128,4,512]{2,1,0:T(4,128)(2,1)} custom-call(s32[1,128]{1,0:T(1,128)} %subtract_bitcast_fusion.pfx_ref, s32[1,128]{1,0:T(1,128)} %bitcast.10, s32[1,128]{1,0:T(1,128)} %bitcast.11, bf16[128,4,512]{2,1,0:T(4,128)(2,1)} %q_ref.1, bf16[2,2,2048,128]{3,2,1,0:T(8,128)(2,1)} %prefix.1, bf16[2,4096,128]{2,1,0:T(8,128)(2,1)} %bitcast.7, ...), custom_call_target="tpu_custom_call" | custom-call | flops 16000000000 | bytes 12000000 | tf_op jit(solution)/shard_map/pallas_call | solution.py:447
  91.3 2.0 %copy.12 = bf16[128,4,512]{2,1,0:T(4,128)(2,1)} copy(bf16[128,4,512]{2,1,0:T(4,128)(2,1)} %shard_map.100) | data formatting | bytes 1048576

commit v2 on v1

--- a/solution.py
+++ b/solution.py
@@ -87,7 +87,7 @@
             ]
 
 
-NMSG = 256
+NMSG = 128
 MESHID = pl.DeviceIdType.MESH
 
 
@@ -111,10 +111,10 @@
 
 
 def mega_kernel(
-    pfx_ref, len_ref, idx_ref, q_ref, prefix, suf, fresh, wo_hbm, a_hbm, b_hbm,
+    pfx_ref, len_ref, idx_ref, q_hbm, prefix, suf_hbm, fresh_hbm, wo_hbm, a_hbm, b_hbm,
     out_ref,
-    kp, vp, pcol, lcol, wo, ag, bg0, bg1, att, fl, fr, fo, part, pr, s1, s2, s3,
-    t2l, t2r, f1l, f3r, idn, idc, acc, cp, cr, cs, cf, xs, e0, e1, ol, orr, eR, eL, dl, dr,
+    q_ref, suf, fresh, kp, vp, pcol, lcol, wo, ag, bg0, bg1, att, fl, fr, fo, part, pr, s1, s2, s3,
+    t2l, t2r, f1l, f3r, idn, idc, acc, cp, cpr, cs, cx, ct, cf, xs, e0, e1, ol, orr, eR, eL, dl, dr,
     lsem, ssem, rsem,
 ):
     a, t = lax.axis_index("adapter"), lax.axis_index("tensor")
@@ -122,11 +122,11 @@
     zr, zl = (((z + 1) % 8) * 4 + y, t), (((z + 7) % 8) * 4 + y, t)
     yr, yl, yo = (z * 4 + (y + 1) % 4, t), (z * 4 + (y + 3) % 4, t), (z * 4 + (y + 2) % 4, t)
     xr, xl, pc = (a, ((x + 1) % 4) * 2 + c), (a, ((x + 3) % 4) * 2 + c), (a, x * 2 + (1 - c))
-    peers = [(a, (t + d) % 8) for d in range(1, 8)]
+    xo = (a, ((x + 2) % 4) * 2 + c)
     net = Net(ssem, rsem)
 
     barrier = pltpu.get_barrier_semaphore()
-    everyone = [zr, zl, yr, yl, yo] + peers
+    everyone = [zr, zl, yr, yl, yo, xr, xl, xo, pc]
     for dev in everyone:
         pl.semaphore_signal(barrier, inc=1, device_id=dev, device_id_type=MESHID)
 
@@ -143,6 +143,9 @@
         for d in loads[name]:
             d.wait()
 
+    load("kv", q_hbm, q_ref)
+    load("kv", suf_hbm, suf)
+    load("kv", fresh_hbm, fresh)
     for which, ref in enumerate((kp, vp)):
         for slot in range(2):
             load("kv", prefix.at[which, slot], ref.at[:, slot * HEAD : (slot + 1) * HEAD])
@@ -184,14 +187,6 @@
         net.copy(idx_ref, idn.at[1], yl),
         net.copy(idx_ref, idn.at[2], yo),
     ]
-    pl.semaphore_wait(barrier, len(everyone))
-    z_first(0)
-    for d in id_msgs:
-        d.start()
-
-    pcol[...] = row_columns(pfx_ref)
-    lcol[...] = row_columns(len_ref)
-    idc[0] = row_columns(idx_ref)
 
     feat = {}
     for m in range(4):
@@ -254,46 +249,45 @@
         lanes = lax.broadcasted_iota(jnp.int32, (1, 128), 1) // 64
         return (lanes + first).astype(F32)
 
-    def codes(b):
-        total = None
+    def codes_part(b, slots, first=False):
+        total = None if first else acc[b]
         ids = idc[b]
-        for d in range(8):
+        for d in slots:
             got = lax.dot_general(feats[b][...], ag[d], NT, preferred_element_type=F32)
             for half in range(2):
                 mine = jnp.where(ids == lane_adapter(2 * d + half), got[:, half * 128 : half * 128 + 128], 0.0)
                 total = mine if total is None else total + mine
-        acc[...] = total
-        folded = acc[...] + pltpu.roll(acc[...], 64, 1)
+        acc[b] = total
+
+    def codes_end(b):
+        folded = acc[b] + pltpu.roll(acc[b], 64, 1)
         cp[b] = jnp.where(lowh, folded[:256], folded[256:]).astype(BF)
-
-    scat, gath = {}, {}
-    for b in range(4):
-        for d in range(1, 8):
-            to = (t + d) % 8
-            rows = pl.ds(pl.multiple_of(to * 32, 32), 32)
-            scat[b, d] = net.copy(cp.at[b, rows], cr.at[b, d], (a, to))
-            rows = pl.ds(pl.multiple_of(t * 32, 32), 32)
-            gath[b, d] = net.copy(cs.at[b], cf.at[b, rows], (a, to))
-
-    def scatter_codes(b):
-        for d in range(1, 8):
-            scat[b, d].start()
-
-    def reduce_codes(b):
-        rows = pl.ds(pl.multiple_of(t * 32, 32), 32)
-        s = cp[b, rows, :].astype(F32)
-        for d in range(1, 8):
-            scat[b, d].wait_recv()
-            s = s + cr[b, d].astype(F32)
+        pair_codes[b].start()
+
+    mine = pl.ds(pl.multiple_of(c * 128, 128), 128)
+    theirs = pl.ds(pl.multiple_of((1 - c) * 128, 128), 128)
+    pair_codes = [net.copy(cp.at[b, theirs], cpr.at[b], pc) for b in range(4)]
+    x_codes = [[net.copy(cs.at[b], cx.at[b, n], dev) for n, dev in enumerate((xr, xl, xo))] for b in range(4)]
+    back_codes = [net.copy(ct.at[b], cf.at[b, mine], pc) for b in range(4)]
+
+    def codes_pair(b):
+        pair_codes[b].wait_recv()
+        cs[b] = (cp[b, mine, :].astype(F32) + cpr[b].astype(F32)).astype(BF)
+        for d in x_codes[b]:
+            d.start()
+
+    def codes_sum(b):
+        s = cs[b].astype(F32)
+        for n, d in enumerate(x_codes[b]):
+            d.wait_recv()
+            s = s + cx[b, n].astype(F32)
         s = s.astype(BF)
-        cs[b] = s
-        cf[b, rows, :] = s
-        for d in range(1, 8):
-            gath[b, d].start()
+        ct[b] = s
+        back_codes[b].start()
+        cf[b, mine, :] = s
 
     def spread_codes(b):
-        for d in range(1, 8):
-            gath[b, d].wait_recv()
+        back_codes[b].wait_recv()
         packed = cf[b].astype(F32)
         turned = pltpu.roll(packed, 64, 1)
         both = jnp.concatenate([jnp.where(lowh, packed, turned), jnp.where(lowh, turned, packed)], axis=0)
@@ -308,8 +302,10 @@
             rows, ha, hb = slice(m * 256, m * 256 + 256), slice(m * 256, m * 256 + 128), slice(m * 256 + 128, m * 256 + 256)
             outs["or", n, m] = net.copy(es[n].at[3, ha], ol.at[n, ha], yr)
             outs["ol", n, m] = net.copy(es[n].at[3, hb], orr.at[n, hb], yl)
-            outs["r", n, m] = net.copy(eR.at[n, rows], dl.at[n, rows], yr)
-            outs["l", n, m] = net.copy(eL.at[n, rows], dr.at[n, rows], yl)
+            outs["ra", n, m] = net.copy(eR.at[n, ha], dl.at[n, ha], yr)
+            outs["rb", n, m] = net.copy(es[n].at[2, hb], dl.at[n, hb], yr)
+            outs["la", n, m] = net.copy(es[n].at[1, ha], dr.at[n, ha], yl)
+            outs["lb", n, m] = net.copy(eL.at[n, hb], dr.at[n, hb], yl)
 
     def expand(n, b):
         for m in range(2):
@@ -320,22 +316,24 @@
             if b == 3:
                 outs["or", n, m].start()
                 outs["ol", n, m].start()
+            if b == 2:
+                outs["rb", n, m].start()
+            if b == 1:
+                outs["la", n, m].start()
 
     def relay(n, m):
         ha, hb = slice(m * 256, m * 256 + 128), slice(m * 256 + 128, m * 256 + 256)
         e = es[n]
         outs["or", n, m].wait_recv()
         eR[n, ha, :] = e[2, ha, :] + ol[n, ha, :]
-        eR[n, hb, :] = e[2, hb, :]
-        outs["r", n, m].start()
+        outs["ra", n, m].start()
         outs["ol", n, m].wait_recv()
-        eL[n, ha, :] = e[1, ha, :]
         eL[n, hb, :] = e[1, hb, :] + orr[n, hb, :]
-        outs["l", n, m].start()
+        outs["lb", n, m].start()
 
     def finish(n, m):
-        outs["r", n, m].wait_recv()
-        outs["l", n, m].wait_recv()
+        for name in ("ra", "rb", "la", "lb"):
+            outs[name, n, m].wait_recv()
         rows = slice(m * 256, m * 256 + 256)
         cols = slice(n * 256, n * 256 + 256)
         total = part[0, 0, rows, cols].astype(F32) + pr[0, rows, cols].astype(F32)
@@ -343,88 +341,126 @@
         delta = es[n][0, rows, :].astype(F32) + dl[n, rows, :].astype(F32) + dr[n, rows, :].astype(F32)
         out_ref[m * 64 : m * 64 + 64, :, cols] = (total + delta).astype(BF).reshape(64, 4, 256)
 
-    loaded("kv")
-    steps = [(0, 0, 1), (0, 1, 1), (0, 0, 2), (0, 1, 2), (0, 0, 3), (0, 1, 3), (0, 0, 4), (0, 1, 4)]
-    for m in range(4):
-        for i in (2 * m, 2 * m + 1):
-            attend_chunk(i * 64, q_ref, kp, vp, suf, fresh, pcol, lcol, att)
-            if i >= 1:
-                z_step(*steps[i - 1])
-            if i == 4:
-                z_first(1)
+    def attend(i):
+        attend_chunk(i * 64, q_ref, kp, vp, suf, fresh, pcol, lcol, att)
+
+    def send_features(m):
         feat["r", m].start()
         feat["l", m].start()
-        if m == 0:
-            loaded("wo")
-        if m >= 1:
-            base_two(m - 1)
-            forward_features(m - 1)
-        project(m)
-        if m >= 1:
-            base_one(m - 1)
-    z_step(*steps[7])
-    z_first(2)
-    base_two(3)
+
+    def z_both(mat, k):
+        z_step(mat, 0, k)
+        z_step(mat, 1, k)
+
+    pcol[...] = row_columns(pfx_ref) - (a * 2).astype(F32)
+    lcol[...] = row_columns(len_ref)
+    idc[0] = row_columns(idx_ref)
+    loaded("kv")
+    attend(0)
+    pl.semaphore_wait(barrier, len(everyone))
+    z_first(0)
+    for d in id_msgs:
+        d.start()
+    attend(1)
+    send_features(0)
+    attend(2)
+    attend(3)
+    send_features(1)
+    attend(4)
+    z_step(0, 0, 1)
+    attend(5)
+    send_features(2)
+    z_step(0, 1, 1)
+    attend(6)
+    forward_features(0)
+    attend(7)
+    send_features(3)
+    z_step(0, 0, 2)
+    loaded("wo")
+    project(0)
+    forward_features(1)
+    z_step(0, 1, 2)
+    project(1)
+    forward_features(2)
+    project(2)
+    base_two(0)
+    z_step(0, 0, 3)
+    project(3)
+    base_two(1)
+    forward_features(3)
+    z_step(0, 1, 3)
+    z_first(1)
     for n, d in enumerate(id_msgs):
         d.wait_recv()
         idc[n + 1] = row_columns(idn.at[n])
-    forward_features(3)
     loaded("a")
-    loaded("b")
-    codes(0)
-    scatter_codes(0)
-    base_one(3)
+    base_one(0)
+    codes_part(0, (0, 1, 7, 2, 6), True)
+    base_one(1)
+    codes_part(1, (0, 1, 7, 2, 6), True)
+    codes_part(2, (0, 1, 7, 2, 6), True)
+    for b in range(3):
+        codes_part(b, (3, 5))
+    z_step(0, 0, 4)
+    z_step(0, 1, 4)
+    codes_part(0, (4,))
+    codes_end(0)
+    codes_part(1, (4,))
+    codes_end(1)
+    codes_pair(0)
+    codes_part(2, (4,))
+    codes_end(2)
+    codes_pair(1)
     z_step(1, 0, 1)
     z_step(1, 1, 1)
-    codes(1)
-    scatter_codes(1)
-    z_step(1, 0, 2)
-    z_step(1, 1, 2)
-    codes(2)
-    scatter_codes(2)
-    reduce_codes(0)
-    z_step(2, 0, 1)
-    z_step(2, 1, 1)
-    reduce_codes(1)
     for m in range(4):
         feat["rr", m].wait_recv()
         feat["ll", m].wait_recv()
-    codes(3)
-    scatter_codes(3)
+    codes_pair(2)
+    codes_part(3, (0, 1, 7, 2, 6, 3, 5, 4), True)
+    codes_end(3)
+    codes_sum(0)
+    codes_pair(3)
+    base_two(2)
+    base_two(3)
+    codes_sum(1)
+    z_both(1, 2)
+    z_first(2)
+    codes_sum(2)
+    loaded("b")
+    spread_codes(0)
+    spread_codes(1)
+    codes_sum(3)
     z_step(1, 0, 3)
+    spread_codes(2)
     z_step(1, 1, 3)
-    reduce_codes(2)
-    z_step(2, 0, 2)
-    z_step(2, 1, 2)
-    spread_codes(0)
-    reduce_codes(3)
-    spread_codes(1)
-    z_step(1, 0, 4)
-    z_step(1, 1, 4)
-    spread_codes(2)
-    z_step(2, 0, 3)
-    z_step(2, 1, 3)
+    z_both(2, 1)
+    base_one(2)
     spread_codes(3)
+    base_one(3)
+    z_both(1, 4)
     expand(0, 3)
+    z_both(2, 2)
     expand(0, 2)
     expand(0, 1)
+    z_both(2, 3)
     relay(0, 0)
     relay(0, 1)
-    z_step(2, 0, 4)
-    z_step(2, 1, 4)
+    expand(0, 0)
+    for m in range(4):
+        base["1r", m].wait_recv()
+        base["1l", m].wait_recv()
+    z_both(2, 4)
     expand(1, 3)
     expand(1, 2)
     expand(1, 1)
+    finish(0, 0)
+    finish(0, 1)
     relay(1, 0)
     relay(1, 1)
-    expand(0, 0)
     expand(1, 0)
-    for m in range(4):
-        base["1r", m].wait_recv()
-        base["1l", m].wait_recv()
-    for n in range(2):
-        for m in range(2):
-            finish(n, m)
+    finish(1, 0)
+    finish(1, 1)
     for d in net.sent:
         d.wait_send()
 
@@ -441,27 +477,28 @@
     adapter_shrink_weight,
     adapter_expand_weight,
 ):
-    local_prefix = rollout_prefix_index - lax.axis_index("adapter") * 2
     vm, anyspec = pl.BlockSpec(memory_space=pltpu.VMEM), pl.BlockSpec(memory_space=pl.ANY)
     V = pltpu.VMEM
     return pl.pallas_call(
         mega_kernel,
         out_shape=jax.ShapeDtypeStruct((128, 4, 512), BF),
-        in_specs=[vm, vm, vm, vm, anyspec, vm, vm, anyspec, anyspec, anyspec],
+        in_specs=[vm, vm, vm] + [anyspec] * 7,
         out_specs=vm,
         scratch_shapes=[
+            V((128, 4, 512), BF), V((2, 4096, 128), BF), V((2, 128, 4, 128), BF),
             V((2048, 256), BF), V((2048, 256), BF), V((512, 128), F32), V((512, 128), F32),
             V((8, 512, 512), BF), V((8, 256, 512), BF), V((8, 256, 256), BF), V((8, 256, 256), BF),
             V((512, 512), BF), V((512, 512), BF), V((512, 512), BF), V((512, 512), BF),
             V((2, 4, 512, 512), BF), V((4, 512, 512), BF),
             V((512, 512), BF), V((512, 512), BF), V((512, 512), BF),
             V((512, 512), BF), V((512, 512), BF), V((512, 512), BF), V((512, 512), BF),
-            V((3, 1, 128), jnp.int32), V((4, 512, 128), F32), V((512, 128), F32),
-            V((4, 256, 128), BF), V((4, 8, 32, 128), BF), V((4, 32, 128), BF), V((4, 256, 128), BF),
+            V((3, 1, 128), jnp.int32), V((4, 512, 128), F32), V((4, 512, 128), F32),
+            V((4, 256, 128), BF), V((4, 128, 128), BF), V((4, 128, 128), BF),
+            V((4, 3, 128, 128), BF), V((4, 128, 128), BF), V((4, 256, 128), BF),
             V((4, 512, 2048), BF),
             V((4, 512, 256), BF), V((4, 512, 256), BF), V((2, 512, 256), BF), V((2, 512, 256), BF),
             V((2, 512, 256), BF), V((2, 512, 256), BF), V((2, 512, 256), BF), V((2, 512, 256), BF),
-            pltpu.SemaphoreType.DMA((16,)),
+            pltpu.SemaphoreType.DMA((18,)),
             pltpu.SemaphoreType.DMA((NMSG,)),
             pltpu.SemaphoreType.DMA((NMSG,)),
         ],
@@ -470,7 +507,7 @@
         ),
         cost_estimate=pl.CostEstimate(flops=16 * 10**9, bytes_accessed=12 * 10**6, transcendentals=4 * 10**6),
     )(
-        local_prefix.reshape(1, 128),
+        rollout_prefix_index.reshape(1, 128),
         rollout_suffix_length.reshape(1, 128),
         rollout_adapter_index.reshape(1, 128),
         queries,

time: 93.4 us -> 79 us (0.85)
  Pallas kernels: 90.1 us -> 76.8 us
  other arithmetic: 1.17 us -> 0 us
    pallas_call x1, Pallas kernels: 90.1 us -> 76.8 us  [local(): pl.pallas_call(mega_kernel, out_shape=jax.ShapeDtypeStruct((128, 4, 512),...]
    reshape x1 -> x0, other arithmetic: 1.17 us -> none  [local(): local_prefix.reshape(1, 128)]
where the time goes in v2:
time: 79 us; the launch traced here: 78.9 us
  Pallas kernels  76.8 us (97%)
  local copies, waits for them, and re-layouts  2.02 us (3%)
    pallas_call x1, Pallas kernels, local(): pl.pallas_call(mega_kernel, out_shape=jax.ShapeDtypeStruct((128, 4, 512),...  76.8 us
    unnamed x1, local copies, waits for them, and re-layouts  2.02 us

profile of v2, /device:TPU:8, one launch (start us, length us, event | category | flops | bytes accessed | tf_op | source)
XLA Modules:
  0.0 78.9 jit_solution(9764356743912619560)
XLA Ops:
  0.0 76.8 %shard_map.100 = bf16[128,4,512]{2,1,0:T(4,128)(2,1)} custom-call(s32[1,128]{1,0:T(1,128)} %bitcast.9, s32[1,128]{1,0:T(1,128)} %bitcast.10, s32[1,128]{1,0:T(1,128)} %bitcast.11, bf16[128,4,512]{2,1,0:T(4,128)(2,1)} %q_hbm.1, bf16[2,2,2048,128]{3,2,1,0:T(8,128)(2,1)} %prefix.1, bf16[2,4096,128]{2,1,0:T(8,128)(2,1)} %bitcast.6, ...), custom_call_target="tpu_custom_call" | custom-call | flops 16000000000 | bytes 12000000 | tf_op jit(solution)/shard_map/pallas_call | solution.py:482
  76.8 2.0 %copy.12 = bf16[128,4,512]{2,1,0:T(4,128)(2,1)} copy(bf16[128,4,512]{2,1,0:T(4,128)(2,1)} %shard_map.100) | data formatting | bytes 1048576

commit v3 on v2

--- a/solution.py
+++ b/solution.py
@@ -339,7 +339,7 @@
         total = part[0, 0, rows, cols].astype(F32) + pr[0, rows, cols].astype(F32)
         total = total + f1l[rows, cols].astype(F32) + f3r[rows, cols].astype(F32)
         delta = es[n][0, rows, :].astype(F32) + dl[n, rows, :].astype(F32) + dr[n, rows, :].astype(F32)
-        out_ref[m * 64 : m * 64 + 64, :, cols] = (total + delta).astype(BF).reshape(64, 4, 256)
+        out_ref[rows, cols] = (total + delta).astype(BF)
 
     def attend(i):
         attend_chunk(i * 64, q_ref, kp, vp, suf, fresh, pcol, lcol, att)
@@ -403,49 +403,53 @@
         codes_part(b, (3, 5))
     z_step(0, 0, 4)
     z_step(0, 1, 4)
+    z_step(1, 0, 1)
     codes_part(0, (4,))
     codes_end(0)
     codes_part(1, (4,))
     codes_end(1)
     codes_pair(0)
+    z_step(1, 1, 1)
     codes_part(2, (4,))
     codes_end(2)
     codes_pair(1)
-    z_step(1, 0, 1)
-    z_step(1, 1, 1)
     for m in range(4):
         feat["rr", m].wait_recv()
         feat["ll", m].wait_recv()
     codes_pair(2)
     codes_part(3, (0, 1, 7, 2, 6, 3, 5, 4), True)
     codes_end(3)
+    z_step(1, 0, 2)
     codes_sum(0)
     codes_pair(3)
     base_two(2)
     base_two(3)
+    z_step(1, 1, 2)
+    z_first(2)
     codes_sum(1)
-    z_both(1, 2)
-    z_first(2)
     codes_sum(2)
     loaded("b")
     spread_codes(0)
+    z_step(1, 0, 3)
     spread_codes(1)
     codes_sum(3)
-    z_step(1, 0, 3)
+    z_step(1, 1, 3)
     spread_codes(2)
-    z_step(1, 1, 3)
-    z_both(2, 1)
+    z_step(2, 0, 1)
     base_one(2)
+    base_one(3)
+    z_step(2, 1, 1)
     spread_codes(3)
-    base_one(3)
     z_both(1, 4)
     expand(0, 3)
-    z_both(2, 2)
+    z_step(2, 0, 2)
     expand(0, 2)
+    z_step(2, 1, 2)
     expand(0, 1)
-    z_both(2, 3)
     relay(0, 0)
+    z_step(2, 0, 3)
     relay(0, 1)
+    z_step(2, 1, 3)
     expand(0, 0)
     for m in range(4):
         base["1r", m].wait_recv()
@@ -481,7 +485,7 @@
     V = pltpu.VMEM
     return pl.pallas_call(
         mega_kernel,
-        out_shape=jax.ShapeDtypeStruct((128, 4, 512), BF),
+        out_shape=jax.ShapeDtypeStruct((512, 512), BF),
         in_specs=[vm, vm, vm] + [anyspec] * 7,
         out_specs=vm,
         scratch_shapes=[
@@ -517,7 +521,7 @@
         output_projection_weight,
         adapter_shrink_weight.reshape(256, 512),
         adapter_expand_weight.reshape(256, 512),
-    )
+    ).reshape(128, 4, 512)
 
 
 def solution(mesh):

time: 79 us -> 77.8 us (0.985)
  Pallas kernels: 76.8 us -> 75.7 us
    unnamed x1 -> x0, local copies, waits for them, and re-layouts: 2.02 us -> none
    reshape x0 -> x1, local copies, waits for them, and re-layouts: none -> 1.96 us  [local(): return pl.pallas_call(mega_kernel, out_shape=jax.ShapeDtypeStruct((512, 5...]
    pallas_call x1, Pallas kernels: 76.8 us -> 75.7 us  [local(): pl.pallas_call(mega_kernel, out_shape=jax.ShapeDtypeStruct((512, 512), BF...]
where the time goes in v3:
time: 77.8 us; the launch traced here: 77.7 us
  Pallas kernels  75.7 us (97%)
  local copies, waits for them, and re-layouts  1.96 us (3%)
    pallas_call x1, Pallas kernels, local(): pl.pallas_call(mega_kernel, out_shape=jax.ShapeDtypeStruct((512, 512), BF...  75.7 us
    reshape x1, local copies, waits for them, and re-layouts, local(): return pl.pallas_call(mega_kernel, out_shape=jax.ShapeDtypeStruct((512, 5...  1.96 us

profile of v3, /device:TPU:8, one launch (start us, length us, event | category | flops | bytes accessed | tf_op | source)
XLA Modules:
  0.0 77.7 jit_solution(2773211379095238660)
XLA Ops:
  0.0 75.7 %shard_map.100 = bf16[512,512]{1,0:T(8,128)(2,1)} custom-call(s32[1,128]{1,0:T(1,128)} %bitcast.9, s32[1,128]{1,0:T(1,128)} %bitcast.10, s32[1,128]{1,0:T(1,128)} %bitcast.11, bf16[128,4,512]{2,1,0:T(4,128)(2,1)} %q_hbm.1, bf16[2,2,2048,128]{3,2,1,0:T(8,128)(2,1)} %prefix.1, bf16[2,4096,128]{2,1,0:T(8,128)(2,1)} %bitcast.6, ...), custom_call_target="tpu_custom_call" | custom-call | flops 16000000000 | bytes 12000000 | tf_op jit(solution)/shard_map/pallas_call | solution.py:486
  75.7 2.0 %reshape.27 = bf16[128,4,512]{2,1,0:T(4,128)(2,1)} reshape(bf16[512,512]{1,0:T(8,128)(2,1)} %shard_map.100) | data formatting | bytes 1048576 | tf_op jit(solution)/shard_map/reshape | solution.py:524
